TPU v7x, 32 devices: a whole 2x2x4 slice. The times are simulated.
32 devices in a mesh: row: 4 (over y, core), col: 8 (over z, x).
Axes of the slice: x: 2, y: 2, z: 4, core: 2. Of those that a mesh axis runs over, the one named last changes fastest.
Arguments:
- front: float32 [12288, 12288], P('row', 'col'), may hold values from -6 to 6
- delayed: float32 [64, 12288], P('col', 'row'), may hold values from -6 to 6
- dest: int32 [64], P('col'), may hold values from 0 to 1023, as said below
- pivots: int32 [1024], replicated, may hold values from 0 to 12287, as said below
- pair_flags: int32 [1024], replicated, may hold values from 0 to 1, as said below
- linv: float32 [4, 256, 256], replicated, as said below
- dinv_diag: float32 [1024], replicated, may hold values from -0.1 to 0.1
- dinv_off: float32 [1024], replicated, may hold values from -0.08 to 0.08
Outputs:
- trailing: float32 [12288, 12288], P('row', 'col')
- factor: float32 [12288, 1024], P('row')
Inputs may be any that keep to these rules, and one draw needn't show every extreme that they name: Distinct front columns; slots p * 256 to (p + 1) * 256 - 1 are panel p's pivots. Each block of 1536 columns held by one index of col contains exactly 128 of them. `pair_flags`: A 1 at slot s joins slots s and s + 1 into one 2x2 block; no two 1s are adjacent and the last slot of a panel holds 0. `dest`: several delayed columns may share a slot. Of the 8 delayed columns held by one index of col, at most 2 go to pivot columns held by the same index of col. `linv`: each panel's matrix is unit lower triangular: ones on the diagonal, zeros above it.
All inputs are finite; a program needn't handle non-finite values.
Results may differ from a plain program's by a relative error of at most 0.00015.
Values sent between devices are 32-bit elements; how exact they have to be, the bound alone decides.
A program may use at most 192 MiB of HBM per device.

v0:
```python
import jax
import jax.numpy as jnp
from jax import lax
from jax.sharding import PartitionSpec as P

CAP = 2
precise = lax.Precision.HIGHEST


def broadcast(block, axis, holder):
    block = jnp.where(lax.axis_index(axis) == holder, block, jnp.zeros_like(block))
    return lax.psum(block, axis)


def pair_scale(scaled, pair_bits, diag_part, off_part):
    coupled = pair_bits.astype(jnp.float32) * off_part
    zero_col = jnp.zeros_like(scaled[:, :1])
    shifted_next = jnp.concatenate([scaled[:, 1:], zero_col], axis=1)
    shifted_prev = jnp.concatenate([zero_col, scaled[:, :-1]], axis=1)
    coupled_prev = jnp.concatenate([jnp.zeros_like(coupled[:1]), coupled[:-1]])
    return scaled * diag_part + shifted_next * coupled + shifted_prev * coupled_prev


def select_columns(matrix, wanted, anchor):
    block_width = matrix.shape[1]
    relative = wanted - anchor
    inside = (relative >= 0) & (relative < block_width)
    clipped = jnp.clip(relative, 0, block_width - 1)
    return jnp.where(inside[None, :], jnp.take(matrix, clipped, axis=1), 0.0)


def select_rows(matrix, wanted, anchor):
    block_height = matrix.shape[0]
    relative = wanted - anchor
    inside = (relative >= 0) & (relative < block_height)
    clipped = jnp.clip(relative, 0, block_height - 1)
    return jnp.where(inside[:, None], jnp.take(matrix, clipped, axis=0), 0.0)


def body(front, delayed, dest, pivots, pair_flags, linv, dinv_diag, dinv_off):
    col_count = lax.axis_size("col")
    rows_blk, cols_blk = front.shape
    row_start = lax.axis_index("row") * rows_blk
    col_start = lax.axis_index("col") * cols_blk
    panel_count = linv.shape[0]
    panel_width = linv.shape[1]
    slot_total = pivots.shape[0]
    slot_ids = jnp.arange(slot_total, dtype=jnp.int32)
    owner_ids = jnp.arange(col_count, dtype=jnp.int32)
    slot_hit = dest[:, None] == slot_ids[None, :]
    targets = jnp.sum(jnp.where(slot_hit, pivots[None, :], 0), axis=1)
    owners = targets // cols_blk
    within = targets - owners * cols_blk
    owner_hit = (owners[:, None] == owner_ids[None, :]).astype(jnp.int32)
    earlier = jnp.cumsum(owner_hit, axis=0) - owner_hit
    rank_in = jnp.sum(earlier * owner_hit, axis=1)
    slot_pos = jnp.arange(CAP, dtype=jnp.int32)
    placed = (owner_hit[:, :, None] > 0) & (rank_in[:, None, None] == slot_pos[None, None, :])
    send_vals = jnp.einsum("kos,kr->osr", placed.astype(jnp.float32), delayed, precision=precise)
    send_cols = jnp.sum(jnp.where(placed, within[:, None, None] + 1, 0), axis=0) - 1
    recv_vals, recv_cols = (
        lax.all_to_all(send_vals, "col", split_axis=0, concat_axis=0, tiled=True),
        lax.all_to_all(send_cols, "col", split_axis=0, concat_axis=0, tiled=True),
    )
    flat_vals = recv_vals.reshape(-1, rows_blk)
    flat_cols = recv_cols.reshape(-1)
    col_ids = jnp.arange(cols_blk, dtype=jnp.int32)
    col_hit = (flat_cols[:, None] == col_ids[None, :]).astype(jnp.float32)
    current = front + lax.dot_general(
        flat_vals, col_hit, (((0,), (0,)), ((), ())), precision=precise
    )
    factors = []
    piv_owner = pivots // cols_blk
    piv_hit = (piv_owner[:, None] == owner_ids[None, :]).astype(jnp.int32)
    piv_rank = jnp.sum((jnp.cumsum(piv_hit, axis=0) - piv_hit) * piv_hit, axis=1)
    per_owner = slot_total // col_count
    owned_here = piv_owner == lax.axis_index("col")
    rank_ids = jnp.arange(per_owner, dtype=jnp.int32)
    own_slots = jnp.sum(
        jnp.where(
            owned_here[None, :] & (piv_rank[None, :] == rank_ids[:, None]), slot_ids[None, :], 0
        ),
        axis=1,
    )
    compact = select_columns(current, pivots[own_slots], col_start)
    gathered = lax.all_gather(compact, "col", axis=1, tiled=True)
    every_panel = jnp.take(gathered, piv_owner * per_owner + piv_rank, axis=1)
    previous = []
    for panel_index in range(panel_count):
        offset = panel_index * panel_width
        panel_cols = every_panel[:, offset : offset + panel_width]
        for cols_before, rows_before in previous:
            panel_cols = panel_cols - lax.dot_general(
                cols_before,
                rows_before[offset : offset + panel_width],
                (((1,), (1,)), ((), ())),
                precision=precise,
            )
        finish_offset = panel_index * panel_width
        finish_scaled = jnp.dot(panel_cols, jnp.transpose(linv[panel_index]), precision=precise)
        finish_columns = pair_scale(
            finish_scaled,
            pair_flags[finish_offset : finish_offset + panel_width],
            dinv_diag[finish_offset : finish_offset + panel_width],
            dinv_off[finish_offset : finish_offset + panel_width],
        )
        root_row = col_start // rows_blk
        slice_start = jnp.clip(col_start - row_start, 0, rows_blk - cols_blk)
        root_piece = lax.dynamic_slice_in_dim(finish_scaled, slice_start, cols_blk, 0)
        col_scaled = broadcast(root_piece, "row", root_row)
        current = current - lax.dot_general(
            finish_columns, col_scaled, (((1,), (1,)), ((), ())), precision=precise
        )
        factors.append(finish_columns)
        if panel_index + 1 < panel_count:
            pivot_part = select_rows(finish_scaled, pivots, row_start)
            pivot_rows = lax.psum(pivot_part, "row")
            previous.append((finish_columns, pivot_rows))
    row_ids = row_start + jnp.arange(rows_blk, dtype=jnp.int32)
    row_in = jnp.any(row_ids[:, None] == pivots[None, :], axis=1)
    col_in = jnp.any((col_start + col_ids)[:, None] == pivots[None, :], axis=1)
    trailing = jnp.where(row_in[:, None] | col_in[None, :], 0.0, current)
    factor = jnp.concatenate(factors, axis=1)
    return (trailing, factor)


def solution(mesh):
    return jax.shard_map(
        body,
        mesh=mesh,
        in_specs=(P("row", "col"), P("col", "row"), P("col"), P(), P(), P(), P(), P()),
        out_specs=(P("row", "col"), P("row", None)),
        check_vma=False,
    )
```

profile of v0, /device:TPU:0, one launch (start us, length us, event | category | flops | bytes accessed | tf_op | source)
XLA Modules:
  0.0 721.7 jit_solution(9475887452106300543)
XLA Ops:
  9.2 7.3 %all-to-all-start.1 = ((s32[8,1,2]{2,1,0:T(1,128)}), s32[8,1,2]{2,1,0:T(1,128)S(1)}, u32[]{:S(2)}, u32[]{:S(2)}) async-start(s32[8,1,2]{2,1,0:T(1,128)} %copy.32), calls=%async_computation.1 | async-start | bytes 8192 | tf_op jit(solution)/shard_map/all_to_all | solution.py:63
  36.8 18.0 %convolution_add_fusion = f32[3072,1536]{1,0:T(8,128)} fusion(f32[3072,1536]{1,0:T(8,128)} %param.10, f32[16,3072]{1,0:T(8,128)S(1)} %reshape.189, s32[16]{0:T(128)S(1)} %eq.152), kind=kOutput, calls=%fused_computation.7 | convolution fusion | flops 910712832 | bytes 37945408 | tf_op jit(solution)/shard_map/dot_general | solution.py:69
  54.8 18.7 %copy.33 = f32[3072,1536]{0,1:T(8,128)} copy(f32[3072,1536]{1,0:T(8,128)} %convolution_add_fusion) | data formatting | bytes 37748736 | tf_op jit(solution)/shard_map/add | solution.py:69
  73.4 8.2 %gather_fusion.1 = f32[128,3072]{1,0:T(8,128)S(1)} fusion(f32[3072,1536]{0,1:T(8,128)} %copy.33, s32[1024]{0:T(1024)S(1)} %pad_clamp_fusion), kind=kCustom, calls=%fused_computation.4 | custom fusion | bytes 3146240 | tf_op jit(solution)/shard_map/jit(_take)/gather | solution.py:29
  84.1 173.5 %all-gather.2.cloned.1.call-done = f32[3072,1024]{0,1:T(8,128)} async-done(((f32[3072,128]{0,1:T(8,128)}), f32[3072,1024]{0,1:T(8,128)}) %all-gather.2.cloned.1.call-update) | async-done | bytes 12582928 | tf_op jit(solution)/shard_map/all_gather | solution.py:86
  257.6 16.5 %gather_fusion.2 = f32[1024,3072]{1,0:T(8,128)} fusion(f32[3072,1024]{0,1:T(8,128)} %all-gather.2.cloned.1.call-done, s32[1024]{0:T(1024)S(1)} %broadcast_clamp_fusion), kind=kCustom, calls=%fused_computation.5 | custom fusion | bytes 25169920 | tf_op jit(solution)/shard_map/jit(_take)/gather | solution.py:87
  274.1 12.6 %copy.34 = f32[1024,3072]{0,1:T(8,128)} copy(f32[1024,3072]{1,0:T(8,128)} %gather_fusion.2) | data formatting | bytes 25165824 | tf_op jit(solution)/shard_map/jit(_take)/gather | solution.py:87
  286.7 12.4 %select_bitcast_fusion = f32[3072,1024]{1,0:T(8,128)} fusion(f32[1024,3072]{0,1:T(8,128)} %copy.34, pred[1024]{0:T(1024)(128)(4,1)S(1)} %compare_and_fusion.2), kind=kLoop, calls=%fused_computation.9 | loop fusion | flops 3145728 | bytes 25166848 | tf_op jit(solution)/shard_map/jit(_take)/select_n | solution.py:87
  324.0 27.4 %all-reduce.14.cloned.1.call-done = f32[1024,256]{1,0:T(8,128)} async-done(((f32[1024,256]{1,0:T(8,128)}), f32[1024,256]{1,0:T(8,128)}) %all-reduce.14.cloned.1.call-update) | async-done | bytes 1048592 | tf_op jit(solution)/shard_map/psum | solution.py:117
  351.4 7.3 %convolution_subtract_fusion.5 = f32[3072,256]{1,0:T(8,128)S(1)} fusion(f32[3072,256]{0,1:T(8,128)S(1)} %multiply_add_fusion.3, f32[3072,1024]{1,0:T(8,128)} %select_bitcast_fusion, f32[1024,256]{1,0:T(8,128)} %all-reduce.14.cloned.1.call-done), kind=kOutput, calls=%fused_computation.17 | convolution fusion | flops 2416705536 | bytes 9699328 | tf_op jit(solution)/shard_map/dot_general | solution.py:93
  387.6 8.0 %convolution_subtract_fusion.4 = f32[3072,256]{1,0:T(8,128)} fusion(f32[3072,256]{0,1:T(8,128)S(1)} %multiply_add_fusion.3, f32[3072,1024]{1,0:T(8,128)} %select_bitcast_fusion, f32[1024,256]{1,0:T(8,128)S(1)} %copy-done.19), kind=kOutput, calls=%fused_computation.16 | convolution fusion | flops 2416705536 | bytes 9699328 | tf_op jit(solution)/shard_map/dot_general | solution.py:93
  397.3 8.3 %convolution_subtract_fusion.2 = f32[3072,256]{1,0:T(8,128)} fusion(f32[3072,256]{0,1:T(8,128)S(1)} %multiply_add_fusion.3, f32[3072,1024]{1,0:T(8,128)} %select_bitcast_fusion, f32[1024,256]{1,0:T(8,128)S(1)} %copy-done.19), kind=kOutput, calls=%fused_computation.14 | convolution fusion | flops 2416705536 | bytes 9699328 | tf_op jit(solution)/shard_map/dot_general | solution.py:93
  405.5 11.8 %all-reduce.16.cloned.1.call-done = f32[1024,256]{1,0:T(8,128)} async-done(((f32[1024,256]{1,0:T(8,128)}), f32[1024,256]{1,0:T(8,128)}) %all-reduce.16.cloned.1.call-update) | async-done | bytes 1048592 | tf_op jit(solution)/shard_map/psum | solution.py:117
  417.3 8.3 %convolution_subtract_fusion.3 = f32[3072,256]{1,0:T(8,128)S(1)} fusion(f32[3072,256]{1,0:T(8,128)} %convolution_subtract_fusion.4, f32[3072,256]{0,1:T(8,128)} %multiply_add_fusion.2, f32[1024,256]{1,0:T(8,128)} %all-reduce.16.cloned.1.call-done), kind=kOutput, calls=%fused_computation.15 | convolution fusion | flops 2416705536 | bytes 9699328 | tf_op jit(solution)/shard_map/dot_general | solution.py:93
  447.7 7.0 multiply_add_fusion.1
  457.2 8.1 %convolution_subtract_fusion.1 = f32[3072,256]{1,0:T(8,128)} fusion(f32[3072,256]{1,0:T(8,128)S(1)} %copy-done.16, f32[3072,256]{0,1:T(8,128)S(1)} %copy-done.8, f32[1024,256]{1,0:T(8,128)} %all-reduce.16.cloned.1.call-done), kind=kOutput, calls=%fused_computation.13 | convolution fusion | flops 2416705536 | bytes 9699328 | tf_op jit(solution)/shard_map/dot_general | solution.py:93
  465.3 19.0 %all-reduce.18.cloned.1.call-done = f32[1024,256]{1,0:T(8,128)} async-done(((f32[1024,256]{1,0:T(8,128)}), f32[1024,256]{1,0:T(8,128)}) %all-reduce.18.cloned.1.call-update) | async-done | bytes 1048592 | tf_op jit(solution)/shard_map/psum | solution.py:117
  484.4 8.3 %convolution_subtract_fusion = f32[3072,256]{1,0:T(8,128)S(1)} fusion(f32[3072,256]{1,0:T(8,128)} %convolution_subtract_fusion.1, f32[3072,256]{0,1:T(8,128)} %multiply_add_fusion.1, f32[1024,256]{1,0:T(8,128)} %all-reduce.18.cloned.1.call-done), kind=kOutput, calls=%fused_computation.12 | convolution fusion | flops 2416705536 | bytes 9699328 | tf_op jit(solution)/shard_map/dot_general | solution.py:93
  517.4 12.6 %copy.38 = f32[3072,1024]{1,0:T(8,128)} copy(f32[3072,1024]{0,1:T(8,128)} %pad_maximum_fusion) | data formatting | bytes 25165824
  530.0 90.6 %all-reduce.20.cloned.1.call-done = (f32[1536,256]{0,1:T(8,128)}, f32[1536,256]{0,1:T(8,128)}, f32[1536,256]{0,1:T(8,128)}, f32[1536,256]{0,1:T(8,128)}) async-done(((f32[1536,256]{0,1:T(8,128)}, f32[1536,256]{0,1:T(8,128)}, f32[1536,256]{0,1:T(8,128)}, f32[1536,256]{0,1:T(8,128)}), (f32[1536,256]{0,1:T(8,128)}, f32[1536,256]{0,1:T(8,128)}, f32[1536,256]{0,1:T(8,128)}, ...) | async-done | bytes 6291472 | tf_op jit(solution)/shard_map/psum | solution.py:12
  620.6 19.9 %fusion.44 = f32[3072,1536]{1,0:T(8,128)} fusion(f32[3072,256]{0,1:T(8,128)} %multiply_add_fusion.1, f32[1536,256]{0,1:T(8,128)} %get-tuple-element.11), kind=kOutput, calls=%fused_computation.119 | convolution fusion | flops 14495514624 | bytes 23592960 | tf_op jit(solution)/shard_map/dot_general | solution.py:111
  640.5 18.5 %fusion.43 = f32[3072,1536]{1,0:T(8,128)} fusion(f32[3072,256]{0,1:T(8,128)S(1)} %copy-done.10, f32[1536,256]{0,1:T(8,128)S(1)} %copy-done.18), kind=kOutput, calls=%fused_computation.118 | convolution fusion | flops 14495514624 | bytes 23592960 | tf_op jit(solution)/shard_map/dot_general | solution.py:111
  659.0 17.9 %fusion.42 = f32[3072,1536]{1,0:T(8,128)} fusion(f32[3072,256]{0,1:T(8,128)S(1)} %multiply_add_fusion.3, f32[1536,256]{0,1:T(8,128)S(1)} %copy-done.17), kind=kOutput, calls=%fused_computation.117 | convolution fusion | flops 14495514624 | bytes 23592960 | tf_op jit(solution)/shard_map/dot_general | solution.py:111
  676.9 38.1 %subtract_select_fusion = f32[3072,1536]{1,0:T(8,128)} fusion(f32[3072,1536]{1,0:T(8,128)} %fusion.44, f32[3072,1536]{1,0:T(8,128)} %fusion.43, f32[3072,1536]{1,0:T(8,128)} %convolution_add_fusion, f32[3072,1536]{1,0:T(8,128)} %fusion.42, f32[3072,256]{0,1:T(8,128)} %copy-done.15, f32[1536,256]{0,1:T(8,128)} %get-tuple-element.14, ...), kind=kOutput, calls=%fused_computation.6 | convolution fusion | flops 14523826176 | bytes 99095040 | tf_op jit(solution)/shard_map/dot_general | solution.py:111
  (126 shorter events, 129.0 us)
Async XLA Ops:
  7.2 9.3 %copy-start = (f32[8,3072]{1,0:T(8,128)S(1)}, f32[8,3072]{1,0:T(8,128)}, u32[]{:S(2)}) copy-start(f32[8,3072]{1,0:T(8,128)} %param.11) | copy-start | bytes 294916
  9.2 13.7 %all-to-all-start.1 = ((s32[8,1,2]{2,1,0:T(1,128)}), s32[8,1,2]{2,1,0:T(1,128)S(1)}, u32[]{:S(2)}, u32[]{:S(2)}) async-start(s32[8,1,2]{2,1,0:T(1,128)} %copy.32), calls=%async_computation.1 | async-start | bytes 8192 | tf_op jit(solution)/shard_map/all_to_all | solution.py:63
  22.9 13.8 %all-to-all-start = ((f32[8,2,3072]{2,1,0:T(2,128)}), f32[8,2,3072]{2,1,0:T(2,128)S(1)}, u32[]{:S(2)}, u32[]{:S(2)}) async-start(f32[8,2,3072]{2,1,0:T(2,128)} %copy.31), calls=%async_computation | async-start | bytes 393216 | tf_op jit(solution)/shard_map/all_to_all | solution.py:62
  28.9 228.7 %all-gather.2.cloned.1.call-start = ((), (), s32[]{:S(2)}) async-start(), calls=%async_computation.2 | async-start | bytes 14155776 | tf_op jit(solution)/shard_map/all_gather | solution.py:86
  81.7 2.3 copy-start.11
  81.7 2.3 copy-start.22
  83.2 268.2 %all-reduce.14.cloned.1.call-start = ((), (), s32[]{:S(2)}) async-start(), calls=%async_computation.3 | async-start | bytes 2097152 | tf_op jit(solution)/shard_map/psum | solution.py:117
  304.0 3.7 copy-start.6
  316.7 100.6 %all-reduce.16.cloned.1.call-start = ((), (), s32[]{:S(2)}) async-start(), calls=%async_computation.4 | async-start | bytes 2097152 | tf_op jit(solution)/shard_map/psum | solution.py:117
  316.9 5.4 copy-start.7
  380.4 103.9 %all-reduce.18.cloned.1.call-start = ((), (), s32[]{:S(2)}) async-start(), calls=%async_computation.5 | async-start | bytes 2097152 | tf_op jit(solution)/shard_map/psum | solution.py:117
  380.7 7.0 copy-start.19
  387.6 8.0 %copy-start.5 = (f32[3072,256]{0,1:T(8,128)S(1)}, f32[3072,256]{0,1:T(8,128)}, u32[]{:S(2)}) copy-start(f32[3072,256]{0,1:T(8,128)} %copy-done.4) | copy-start | bytes 9437188
  447.5 173.2 %all-reduce.20.cloned.1.call-start = ((), (), s32[]{:S(2)}) async-start(), calls=%async_computation.6 | async-start | bytes 12582912 | tf_op jit(solution)/shard_map/psum | solution.py:12
  447.7 7.1 copy-start.3
  447.7 8.7 %copy-start.16 = (f32[3072,256]{1,0:T(8,128)S(1)}, f32[3072,256]{1,0:T(8,128)}, u32[]{:S(2)}) copy-start(f32[3072,256]{1,0:T(8,128)} %convolution_subtract_fusion.2) | copy-start | bytes 9437188
  454.7 2.5 copy-start.8
  503.4 4.6 copy-start.13
  508.0 3.0 copy-start.9
  508.0 4.0 copy-start.14
  620.6 19.9 %copy-start.10 = (f32[3072,256]{0,1:T(8,128)S(1)}, f32[3072,256]{0,1:T(8,128)}, u32[]{:S(2)}) copy-start(f32[3072,256]{0,1:T(8,128)} %multiply_add_fusion.2) | copy-start | bytes 9437188
  620.6 19.9 %copy-start.18 = (f32[1536,256]{0,1:T(8,128)S(1)}, f32[1536,256]{0,1:T(8,128)}, u32[]{:S(2)}) copy-start(f32[1536,256]{0,1:T(8,128)} %get-tuple-element.12) | copy-start | bytes 4718596
  640.5 18.5 %copy-start.17 = (f32[1536,256]{0,1:T(8,128)S(1)}, f32[1536,256]{0,1:T(8,128)}, u32[]{:S(2)}) copy-start(f32[1536,256]{0,1:T(8,128)} %get-tuple-element.13) | copy-start | bytes 4718596
  676.9 38.1 %copy-start.1 = (f32[8,3072]{1,0:T(8,128)S(1)}, f32[8,3072]{1,0:T(8,128)}, u32[]{:S(2)}) copy-start(f32[8,3072]{1,0:T(8,128)} %param.11) | copy-start | bytes 294916
  (6 other events, 10.8 us)
Sparse Core Ops, SparseCore 0:
  83.3 174.2 all-gather.1
  316.8 34.4 all-reduce.13
  380.5 36.7 all-reduce.15
  447.6 36.7 all-reduce.17
  500.5 120.0 all-reduce.19
where the time goes:
time: 728 us; the launch traced here: 722 us
  waiting for transfers between devices  329 us (45%)
  matrix products  178 us (24%)
  local copies, waits for them, and re-layouts  124 us (17%)
  other arithmetic  61.7 us (8%)
  starting transfers between devices  14.6 us (2%)
  between operations  14.4 us (2%)
    all_gather x1, waiting for transfers between devices, body(): gathered = lax.all_gather(compact, 'col', axis=1, tiled=True)  174 us
    dot_general x4, matrix products, body(): lax.dot_general(finish_columns, col_scaled, (((1,), (1,)), ((), ())), pre...  94.3 us
    psum x1, waiting for transfers between devices, broadcast(): return lax.psum(block, axis)  90.6 us
    psum x3, waiting for transfers between devices, body(): pivot_rows = lax.psum(pivot_part, 'row')  58.2 us
    dot_general x6, matrix products, body(): lax.dot_general(cols_before, rows_before[offset:offset + panel_width], ((...  48.4 us
    gather x2, local copies, waits for them, and re-layouts, body(): every_panel = jnp.take(gathered, piv_owner * per_owner + piv_rank, axis=1)  29.1 us
    unnamed x47, local copies, waits for them, and re-layouts  21.9 us
    add x4, other arithmetic, pair_scale(): scaled * diag_part + shifted_next * coupled + shifted_prev * coupled_prev  20.7 us
  transfers between devices with their start and end apart: 7, of which 6 were waited for; matrix products, arithmetic and copies ran while one was open for 11% of the time, Pallas kernels for 0%

commit v1 on v0

--- a/solution.py
+++ b/solution.py
@@ -83,7 +83,9 @@
         axis=1,
     )
     compact = select_columns(current, pivots[own_slots], col_start)
-    gathered = lax.all_gather(compact, "col", axis=1, tiled=True)
+    gathered = jnp.concatenate(
+        lax.all_to_all(jnp.stack([compact] * lax.axis_size("col")), "col", 0, 0), axis=1
+    )
     every_panel = jnp.take(gathered, piv_owner * per_owner + piv_rank, axis=1)
     previous = []
     for panel_index in range(panel_count):

time: 728 us -> 837 us (1.15)
  waiting for transfers between devices: 329 us -> 427 us
    all_to_all x0 -> x1, waiting for transfers between devices: none -> 270 us  [body(): lax.all_to_all(jnp.stack([compact] * lax.axis_size('col')), 'col', 0, 0)]
    all_gather x1 -> x0, waiting for transfers between devices: 174 us -> none  [body(): gathered = lax.all_gather(compact, 'col', axis=1, tiled=True)]
  transfers between devices with their start and end apart: 7 -> 7, of which waited for: 6 -> 6; matrix products, arithmetic and copies ran while one was open for 11% -> 10% of each run, Pallas kernels for 0% -> 0%
where the time goes in v1:
time: 837 us; the launch traced here: 830 us
  waiting for transfers between devices  427 us (51%)
  matrix products  178 us (21%)
  local copies, waits for them, and re-layouts  130 us (16%)
  other arithmetic  60.1 us (7%)
  starting transfers between devices  20 us (2%)
  between operations  14.4 us (2%)
    all_to_all x1, waiting for transfers between devices, body(): lax.all_to_all(jnp.stack([compact] * lax.axis_size('col')), 'col', 0, 0)  270 us
    dot_general x4, matrix products, body(): lax.dot_general(finish_columns, col_scaled, (((1,), (1,)), ((), ())), pre...  94.3 us
    psum x1, waiting for transfers between devices, broadcast(): return lax.psum(block, axis)  90.9 us
    psum x3, waiting for transfers between devices, body(): pivot_rows = lax.psum(pivot_part, 'row')  59.2 us
    dot_general x6, matrix products, body(): lax.dot_general(cols_before, rows_before[offset:offset + panel_width], ((...  48.3 us
    gather x2, local copies, waits for them, and re-layouts, body(): every_panel = jnp.take(gathered, piv_owner * per_owner + piv_rank, axis=1)  29.1 us
    unnamed x47, local copies, waits for them, and re-layouts  21.9 us
    add x4, other arithmetic, pair_scale(): scaled * diag_part + shifted_next * coupled + shifted_prev * coupled_prev  20.5 us
  transfers between devices with their start and end apart: 7, of which 6 were waited for; matrix products, arithmetic and copies ran while one was open for 10% of the time, Pallas kernels for 0%

profile of v1, /device:TPU:0, one launch (start us, length us, event | category | flops | bytes accessed | tf_op | source)
XLA Modules:
  0.0 829.8 jit_solution(12624039342449714555)
XLA Ops:
  9.2 7.3 all-to-all-start.1
  36.8 18.0 %convolution_add_fusion = f32[3072,1536]{1,0:T(8,128)} fusion(f32[3072,1536]{1,0:T(8,128)} %param.10, f32[16,3072]{1,0:T(8,128)S(1)} %reshape.215, s32[16]{0:T(128)S(1)} %eq.152), kind=kOutput, calls=%fused_computation.7 | convolution fusion | flops 910712832 | bytes 37945408 | tf_op jit(solution)/shard_map/dot_general | solution.py:69
  54.8 18.7 %copy.33 = f32[3072,1536]{0,1:T(8,128)} copy(f32[3072,1536]{1,0:T(8,128)} %convolution_add_fusion) | data formatting | bytes 37748736 | tf_op jit(solution)/shard_map/add | solution.py:69
  73.4 8.2 gather_fusion.1
  94.7 270.3 %all-to-all-done.2 = f32[8,3072,128]{1,2,0:T(8,128)} async-done(((f32[8,3072,128]{1,2,0:T(8,128)}), f32[8,3072,128]{1,2,0:T(8,128)}, u32[]{:S(2)}, u32[]{:S(2)}) %all-to-all-start.2) | async-done | bytes 12582944 | tf_op jit(solution)/shard_map/all_to_all | solution.py:87
  365.0 16.5 %gather_fusion.2 = f32[1024,3072]{1,0:T(8,128)} fusion(f32[3072,1024]{0,1:T(8,128)} %bitcast.10, s32[1024]{0:T(1024)S(1)} %broadcast_clamp_fusion), kind=kCustom, calls=%fused_computation.5 | custom fusion | bytes 25169920 | tf_op jit(solution)/shard_map/jit(_take)/gather | solution.py:89
  381.5 12.6 %copy.34 = f32[1024,3072]{0,1:T(8,128)} copy(f32[1024,3072]{1,0:T(8,128)} %gather_fusion.2) | data formatting | bytes 25165824 | tf_op jit(solution)/shard_map/jit(_take)/gather | solution.py:89
  394.1 12.4 %select_bitcast_fusion = f32[3072,1024]{1,0:T(8,128)} fusion(f32[1024,3072]{0,1:T(8,128)} %copy.34, pred[1024]{0:T(1024)(128)(4,1)S(1)} %compare_and_fusion.2), kind=kLoop, calls=%fused_computation.9 | loop fusion | flops 3145728 | bytes 25166848 | tf_op jit(solution)/shard_map/jit(_take)/select_n | solution.py:89
  431.2 28.4 %all-reduce.14.cloned.1.call-done = f32[1024,256]{1,0:T(8,128)} async-done(((f32[1024,256]{1,0:T(8,128)}), f32[1024,256]{1,0:T(8,128)}) %all-reduce.14.cloned.1.call-update) | async-done | bytes 1048592 | tf_op jit(solution)/shard_map/psum | solution.py:119
  459.6 7.3 convolution_subtract_fusion.5
  495.9 8.0 convolution_subtract_fusion.4
  505.5 8.2 convolution_subtract_fusion.2
  513.8 11.8 %all-reduce.16.cloned.1.call-done = f32[1024,256]{1,0:T(8,128)} async-done(((f32[1024,256]{1,0:T(8,128)}), f32[1024,256]{1,0:T(8,128)}) %all-reduce.16.cloned.1.call-update) | async-done | bytes 1048592 | tf_op jit(solution)/shard_map/psum | solution.py:119
  525.6 8.3 %convolution_subtract_fusion.3 = f32[3072,256]{1,0:T(8,128)S(1)} fusion(f32[3072,256]{1,0:T(8,128)} %convolution_subtract_fusion.4, f32[3072,256]{0,1:T(8,128)} %multiply_add_fusion.2, f32[1024,256]{1,0:T(8,128)} %all-reduce.16.cloned.1.call-done), kind=kOutput, calls=%fused_computation.15 | convolution fusion | flops 2416705536 | bytes 9699328 | tf_op jit(solution)/shard_map/dot_general | solution.py:95
  555.9 7.0 multiply_add_fusion.1
  565.4 8.1 convolution_subtract_fusion.1
  573.5 19.0 %all-reduce.18.cloned.1.call-done = f32[1024,256]{1,0:T(8,128)} async-done(((f32[1024,256]{1,0:T(8,128)}), f32[1024,256]{1,0:T(8,128)}) %all-reduce.18.cloned.1.call-update) | async-done | bytes 1048592 | tf_op jit(solution)/shard_map/psum | solution.py:119
  592.5 8.3 %convolution_subtract_fusion = f32[3072,256]{1,0:T(8,128)S(1)} fusion(f32[3072,256]{1,0:T(8,128)} %convolution_subtract_fusion.1, f32[3072,256]{0,1:T(8,128)} %multiply_add_fusion.1, f32[1024,256]{1,0:T(8,128)} %all-reduce.18.cloned.1.call-done), kind=kOutput, calls=%fused_computation.12 | convolution fusion | flops 2416705536 | bytes 9699328 | tf_op jit(solution)/shard_map/dot_general | solution.py:95
  625.3 12.6 %copy.38 = f32[3072,1024]{1,0:T(8,128)} copy(f32[3072,1024]{0,1:T(8,128)} %pad_maximum_fusion) | data formatting | bytes 25165824
  637.9 90.9 %all-reduce.20.cloned.1.call-done = (f32[1536,256]{0,1:T(8,128)}, f32[1536,256]{0,1:T(8,128)}, f32[1536,256]{0,1:T(8,128)}, f32[1536,256]{0,1:T(8,128)}) async-done(((f32[1536,256]{0,1:T(8,128)}, f32[1536,256]{0,1:T(8,128)}, f32[1536,256]{0,1:T(8,128)}, f32[1536,256]{0,1:T(8,128)}), (f32[1536,256]{0,1:T(8,128)}, f32[1536,256]{0,1:T(8,128)}, f32[1536,256]{0,1:T(8,128)}, ...) | async-done | bytes 6291472 | tf_op jit(solution)/shard_map/psum | solution.py:12
  728.8 19.9 %fusion.44 = f32[3072,1536]{1,0:T(8,128)} fusion(f32[3072,256]{0,1:T(8,128)} %multiply_add_fusion.1, f32[1536,256]{0,1:T(8,128)} %get-tuple-element.11), kind=kOutput, calls=%fused_computation.119 | convolution fusion | flops 14495514624 | bytes 23592960 | tf_op jit(solution)/shard_map/dot_general | solution.py:113
  748.6 18.5 %fusion.43 = f32[3072,1536]{1,0:T(8,128)} fusion(f32[3072,256]{0,1:T(8,128)S(1)} %copy-done.10, f32[1536,256]{0,1:T(8,128)S(1)} %copy-done.18), kind=kOutput, calls=%fused_computation.118 | convolution fusion | flops 14495514624 | bytes 23592960 | tf_op jit(solution)/shard_map/dot_general | solution.py:113
  767.1 17.9 %fusion.42 = f32[3072,1536]{1,0:T(8,128)} fusion(f32[3072,256]{0,1:T(8,128)S(1)} %multiply_add_fusion.3, f32[1536,256]{0,1:T(8,128)S(1)} %copy-done.17), kind=kOutput, calls=%fused_computation.117 | convolution fusion | flops 14495514624 | bytes 23592960 | tf_op jit(solution)/shard_map/dot_general | solution.py:113
  785.1 38.0 %subtract_select_fusion = f32[3072,1536]{1,0:T(8,128)} fusion(f32[3072,1536]{1,0:T(8,128)} %fusion.44, f32[3072,1536]{1,0:T(8,128)} %fusion.43, f32[3072,1536]{1,0:T(8,128)} %convolution_add_fusion, f32[3072,1536]{1,0:T(8,128)} %fusion.42, f32[3072,256]{0,1:T(8,128)} %copy-done.15, f32[1536,256]{0,1:T(8,128)} %get-tuple-element.14, ...), kind=kOutput, calls=%fused_computation.6 | convolution fusion | flops 14523826176 | bytes 99095040 | tf_op jit(solution)/shard_map/dot_general | solution.py:113
  (126 shorter events, 139.1 us)
Async XLA Ops:
  7.2 9.3 %copy-start = (f32[8,3072]{1,0:T(8,128)S(1)}, f32[8,3072]{1,0:T(8,128)}, u32[]{:S(2)}) copy-start(f32[8,3072]{1,0:T(8,128)} %param.11) | copy-start | bytes 294916
  9.2 13.7 %all-to-all-start.1 = ((s32[8,1,2]{2,1,0:T(1,128)}), s32[8,1,2]{2,1,0:T(1,128)S(1)}, u32[]{:S(2)}, u32[]{:S(2)}) async-start(s32[8,1,2]{2,1,0:T(1,128)} %copy.32), calls=%async_computation.1 | async-start | bytes 8192 | tf_op jit(solution)/shard_map/all_to_all | solution.py:63
  22.9 13.8 %all-to-all-start = ((f32[8,2,3072]{2,1,0:T(2,128)}), f32[8,2,3072]{2,1,0:T(2,128)S(1)}, u32[]{:S(2)}, u32[]{:S(2)}) async-start(f32[8,2,3072]{2,1,0:T(2,128)} %copy.31), calls=%async_computation | async-start | bytes 393216 | tf_op jit(solution)/shard_map/all_to_all | solution.py:62
  88.3 6.1 copy-start.20
  88.3 6.1 copy-start.21
  88.3 6.3 copy-start.11
  88.3 6.3 copy-start.22
  88.3 276.7 %all-to-all-start.2 = ((f32[8,3072,128]{1,2,0:T(8,128)}), f32[8,3072,128]{1,2,0:T(8,128)}, u32[]{:S(2)}, u32[]{:S(2)}) async-start(f32[8,3072,128]{1,2,0:T(8,128)} %stack.2), calls=%async_computation.2 | async-start | bytes 25165824 | tf_op jit(solution)/shard_map/all_to_all | solution.py:87
  93.8 365.8 %all-reduce.14.cloned.1.call-start = ((), (), s32[]{:S(2)}) async-start(), calls=%async_computation.3 | async-start | bytes 2097152 | tf_op jit(solution)/shard_map/psum | solution.py:119
  411.4 3.7 copy-start.6
  424.1 101.5 %all-reduce.16.cloned.1.call-start = ((), (), s32[]{:S(2)}) async-start(), calls=%async_computation.4 | async-start | bytes 2097152 | tf_op jit(solution)/shard_map/psum | solution.py:119
  424.3 5.2 copy-start.7
  488.7 103.9 %all-reduce.18.cloned.1.call-start = ((), (), s32[]{:S(2)}) async-start(), calls=%async_computation.5 | async-start | bytes 2097152 | tf_op jit(solution)/shard_map/psum | solution.py:119
  488.9 7.0 copy-start.19
  495.9 8.0 copy-start.5
  555.6 173.1 %all-reduce.20.cloned.1.call-start = ((), (), s32[]{:S(2)}) async-start(), calls=%async_computation.6 | async-start | bytes 12582912 | tf_op jit(solution)/shard_map/psum | solution.py:12
  555.9 7.1 copy-start.3
  555.9 8.7 %copy-start.16 = (f32[3072,256]{1,0:T(8,128)S(1)}, f32[3072,256]{1,0:T(8,128)}, u32[]{:S(2)}) copy-start(f32[3072,256]{1,0:T(8,128)} %convolution_subtract_fusion.2) | copy-start | bytes 9437188
  611.6 4.6 copy-start.13
  616.2 4.0 copy-start.14
  728.8 19.9 %copy-start.10 = (f32[3072,256]{0,1:T(8,128)S(1)}, f32[3072,256]{0,1:T(8,128)}, u32[]{:S(2)}) copy-start(f32[3072,256]{0,1:T(8,128)} %multiply_add_fusion.2) | copy-start | bytes 9437188
  728.8 19.9 %copy-start.18 = (f32[1536,256]{0,1:T(8,128)S(1)}, f32[1536,256]{0,1:T(8,128)}, u32[]{:S(2)}) copy-start(f32[1536,256]{0,1:T(8,128)} %get-tuple-element.12) | copy-start | bytes 4718596
  748.6 18.5 %copy-start.17 = (f32[1536,256]{0,1:T(8,128)S(1)}, f32[1536,256]{0,1:T(8,128)}, u32[]{:S(2)}) copy-start(f32[1536,256]{0,1:T(8,128)} %get-tuple-element.13) | copy-start | bytes 4718596
  785.1 38.1 %copy-start.1 = (f32[8,3072]{1,0:T(8,128)S(1)}, f32[8,3072]{1,0:T(8,128)}, u32[]{:S(2)}) copy-start(f32[8,3072]{1,0:T(8,128)} %param.11) | copy-start | bytes 294916
  (6 other events, 12.1 us)
Sparse Core Ops, SparseCore 0:
  424.2 35.3 all-reduce.13
  488.8 36.7 all-reduce.15
  555.8 36.7 all-reduce.17
  608.6 120.0 all-reduce.19
